TPU v7x, 128 devices: a whole 4x4x4 slice. The times are simulated.
128 devices in a mesh: dom: 16 (over x, y), blk: 8 (over z, core).
Axes of the slice: x: 4, y: 4, z: 4, core: 2. Of those that a mesh axis runs over, the one named last changes fastest.
Arguments:
- node_features: bfloat16 [32768, 512], P(('dom', 'blk')), may hold values from -6 to 6
- norm_gain: float32 [512], replicated, may hold values from 0.25 to 1.75
- w_query: bfloat16 [512, 512], replicated, may hold values from -0.25 to 0.25
- w_key: bfloat16 [512, 512], replicated, may hold values from -0.25 to 0.25
- w_value: bfloat16 [512, 512], replicated, may hold values from -0.25 to 0.25
- w_out: bfloat16 [512, 512], replicated, may hold values from -1.5 to 1.5
- w_message: bfloat16 [512, 512], replicated, may hold values from -1 to 1
- node_cluster: int32 [32768], P(('dom', 'blk')), may hold values from 0 to 15
- block_pattern: int32 [128, 8], P(('dom', 'blk')), may hold values from 0 to 1, as said below
- send_rows: int32 [2048, 128], P(('dom', 'blk')), may hold values from 0 to 255
- send_counts: int32 [2048], P(('dom', 'blk')), may hold values from 32 to 128, as said below
- edge_src: int32 [524288], P(('dom', 'blk')), may hold values from 0 to 2047
- edge_dst: int32 [524288], P(('dom', 'blk')), may hold values from 0 to 255
- out_grad: bfloat16 [32768, 512], P(('dom', 'blk')), may hold values from -6 to 6
Outputs:
- layer_out: bfloat16 [32768, 512], P(('dom', 'blk'))
- feature_grad: bfloat16 [32768, 512], P(('dom', 'blk'))
- weight_grads: float32 [5, 512, 512], replicated
- gain_grad: float32 [512], replicated
Inputs may be any that keep to these rules, and one draw needn't show every extreme that they name: `block_pattern`: row g has a 1 at column (g mod 8); other entries are 0 or 1. `send_counts`: entry g * 16 + p is how many leading slots of device g's block to dom peer p are live; every device has one peer whose block has all 128 slots live.
All inputs are finite; a program needn't handle non-finite values.
Results may differ from a plain program's by a relative error of at most 0.013.
Values may be sent and summed in bfloat16 or wider, within the bound.
No kernel may reach another device: no remote copies, remote signals or barrier semaphores. Data moves between devices by JAX's collectives and lax.ppermute only.
A program may use at most 128 MiB of HBM per device.

v0:
```python
from functools import partial
import jax
import jax.numpy as jnp
from jax import lax
from jax.sharding import PartitionSpec as P

HEADS = 8
HEAD_DIM = 64
epsilon = 1e-06
score_shift = 8.0


def settle(array):
    return lax.optimization_barrier(array.astype(jnp.bfloat16)).astype(jnp.float32)


def rms_norm(features, norm_gain):
    scaling = lax.rsqrt(jnp.mean(features * features, axis=-1, keepdims=True) + epsilon)
    return features * scaling * norm_gain


def head_norm(projected):
    head_view = projected.reshape(projected.shape[0], HEADS, HEAD_DIM)
    scaling = lax.rsqrt(jnp.mean(head_view * head_view, axis=-1, keepdims=True) + epsilon)
    return (head_view * scaling).reshape(projected.shape)


def block_weights(query_heads, key_heads, allowed):
    scaling = score_shift / HEAD_DIM
    scores = (
        jnp.einsum("rhe,khe->hrk", query_heads, key_heads, preferred_element_type=jnp.float32)
        * scaling
    )
    return jnp.where(allowed[None], jnp.exp(scores - score_shift), 0.0)


def attend_piece(running, shard_piece, offset, query_heads, query_labels, pattern_row, skip_empty):
    key_rows, value_rows, key_labels = shard_piece
    row_count = query_heads.shape[0]
    piece_rows = key_rows.shape[0]
    part_count = max(piece_rows // row_count, 1)
    block_index = jnp.arange(pattern_row.shape[0], dtype=jnp.int32)
    for position in range(part_count):
        first_row = position * piece_rows // part_count
        last_row = (position + 1) * piece_rows // part_count
        part_rows = last_row - first_row
        key_part = key_rows[first_row:last_row].reshape(part_rows, HEADS, HEAD_DIM)
        value_part = value_rows[first_row:last_row].reshape(part_rows, HEADS, HEAD_DIM)
        label_part = key_labels[first_row:last_row]
        owners = (offset + first_row + jnp.arange(part_rows, dtype=jnp.int32)) // row_count
        block_flags = jnp.sum(
            jnp.where(owners[:, None] == block_index[None, :], pattern_row[None, :], 0), axis=1
        )
        allowed = (query_labels[:, None] == label_part[None, :]) & (block_flags[None, :] == 1)

        def accumulate(current, key_part=key_part, value_part=value_part, allowed=allowed):
            numer, denom = current
            weights = block_weights(query_heads, key_part, allowed)
            denom = denom + jnp.sum(weights, axis=2).T
            numer = numer + jnp.einsum(
                "hrk,khe->rhe",
                weights.astype(jnp.bfloat16),
                value_part,
                preferred_element_type=jnp.float32,
            )
            return (numer, denom)

        running = accumulate(running)
    return running


def pair_gradients(query_heads, grad_heads, correction, key_part, value_part, allowed):
    scaling = score_shift / HEAD_DIM
    weights = block_weights(query_heads, key_part, allowed)
    grad_dots = jnp.einsum(
        "rhe,khe->hrk", grad_heads, value_part, preferred_element_type=jnp.float32
    )
    slopes = (weights * (grad_dots - correction.T[:, :, None])).astype(jnp.bfloat16)
    dq_part = (
        jnp.einsum("hrk,khe->rhe", slopes, key_part, preferred_element_type=jnp.float32) * scaling
    )
    dk_part = (
        jnp.einsum("hrk,rhe->khe", slopes, query_heads, preferred_element_type=jnp.float32)
        * scaling
    )
    dv_part = jnp.einsum(
        "hrk,rhe->khe", weights.astype(jnp.bfloat16), grad_heads, preferred_element_type=jnp.float32
    )
    return (dq_part, dk_part, dv_part)


def key_block(
    query_heads, grad_heads, correction, query_labels, skip_empty, dq_total, block_inputs
):
    key_part, value_part, label_part, block_flag = block_inputs
    row_count = query_heads.shape[0]
    allowed = (query_labels[:, None] == label_part[None, :]) & (block_flag == 1)
    dq_part, dk_part, dv_part = pair_gradients(
        query_heads, grad_heads, correction, key_part, value_part, allowed
    )
    flat_terms = (dk_part.reshape(row_count, -1), dv_part.reshape(row_count, -1))
    return (dq_total + settle(dq_part), flat_terms)


def local(
    node_features,
    norm_gain,
    w_query,
    w_key,
    w_value,
    w_out,
    w_message,
    node_cluster,
    block_pattern,
    send_rows,
    send_counts,
    edge_src,
    edge_dst,
    out_grad,
):
    row_count = node_features.shape[0]
    feat_width = node_features.shape[1]
    peer_count = lax.axis_size("dom")
    block_count = lax.axis_size("blk")
    slot_count = send_rows.shape[1]
    features = node_features.astype(jnp.float32)
    normed_f, norm_pull = jax.vjp(rms_norm, features, norm_gain)
    normed = normed_f.astype(jnp.bfloat16)
    live_slots = jnp.arange(slot_count, dtype=jnp.int32)[None, :] < send_counts[:, None]
    outgoing = jnp.where(live_slots[:, :, None], normed[send_rows], jnp.zeros((), jnp.bfloat16))
    incoming = lax.all_to_all(outgoing, "dom", split_axis=0, concat_axis=0, tiled=True)
    query_f, query_pull = jax.vjp(
        head_norm, jnp.dot(normed, w_query, preferred_element_type=jnp.float32)
    )
    key_f, key_pull = jax.vjp(head_norm, jnp.dot(normed, w_key, preferred_element_type=jnp.float32))
    queries = query_f.astype(jnp.bfloat16)
    key_flat = key_f.astype(jnp.bfloat16)
    value_flat = jnp.dot(normed, w_value, preferred_element_type=jnp.float32).astype(jnp.bfloat16)
    query_heads = queries.reshape(row_count, HEADS, HEAD_DIM)
    pattern_row = block_pattern[0]
    start_state = (
        jnp.zeros((row_count, HEADS, HEAD_DIM), jnp.float32),
        jnp.zeros((row_count, HEADS), jnp.float32),
    )
    fold_step = partial(
        attend_piece,
        query_heads=query_heads,
        query_labels=node_cluster,
        pattern_row=pattern_row,
        skip_empty=False,
    )
    key_set = None
    key_set = (
        lax.all_gather(key_flat, "blk", axis=0, tiled=True),
        lax.all_gather(value_flat, "blk", axis=0, tiled=True),
        lax.all_gather(node_cluster, "blk", axis=0, tiled=True),
    )
    numer, denom = fold_step(start_state, key_set, 0)
    slot_table = incoming.reshape(peer_count * slot_count, feat_width)
    pair_index = edge_src * row_count + edge_dst
    edge_counts = jnp.zeros((peer_count * slot_count * row_count,), jnp.int32).at[pair_index].add(1)
    edge_counts = edge_counts.reshape(peer_count * slot_count, row_count).astype(jnp.bfloat16)
    degree = jnp.maximum(
        jax.ops.segment_sum(jnp.ones(edge_dst.shape, jnp.float32), edge_dst, row_count), 1.0
    )
    neighbour_sum = jnp.einsum(
        "sr,sd->rd", edge_counts, slot_table, preferred_element_type=jnp.float32
    )
    mean_rows = (neighbour_sum / degree[:, None]).astype(jnp.bfloat16)
    local_term = jnp.dot(mean_rows, w_message, preferred_element_type=jnp.float32)
    attn_heads = (numer / denom[..., None]).astype(jnp.bfloat16)
    attn_rows = attn_heads.reshape(row_count, feat_width)
    attn_proj = jnp.dot(attn_rows, w_out, preferred_element_type=jnp.float32)
    layer_out = (features + local_term + attn_proj).astype(jnp.bfloat16)
    grad_attn = jnp.einsum(
        "rd,ed->re", out_grad, w_out, preferred_element_type=jnp.float32
    ).reshape(row_count, HEADS, HEAD_DIM)
    grad_heads = (grad_attn / denom[..., None]).astype(jnp.bfloat16)
    correction = jnp.sum(grad_attn * attn_heads.astype(jnp.float32), axis=-1) / denom
    key_rows, value_rows, key_labels = key_set
    block_inputs = (
        key_rows.reshape(block_count, row_count, HEADS, HEAD_DIM),
        value_rows.reshape(block_count, row_count, HEADS, HEAD_DIM),
        key_labels.reshape(block_count, row_count),
        pattern_row,
    )
    block_step = partial(key_block, query_heads, grad_heads, correction, node_cluster, False)
    dq_heads, (key_terms, value_terms) = lax.scan(
        block_step, jnp.zeros((row_count, HEADS, HEAD_DIM), jnp.float32), block_inputs
    )
    key_grad, value_grad = (
        lax.psum_scatter(
            key_terms.reshape(block_count * row_count, feat_width).astype(jnp.bfloat16),
            "blk",
            scatter_dimension=0,
            tiled=True,
        ).astype(jnp.float32),
        lax.psum_scatter(
            value_terms.reshape(block_count * row_count, feat_width).astype(jnp.bfloat16),
            "blk",
            scatter_dimension=0,
            tiled=True,
        ).astype(jnp.float32),
    )
    dq_flat = dq_heads.reshape(row_count, feat_width)
    dquery = query_pull(dq_flat)[0].astype(jnp.bfloat16)
    dkey = key_pull(key_grad)[0].astype(jnp.bfloat16)
    dvalue = value_grad.astype(jnp.bfloat16)
    dmessage = (
        jnp.einsum("rd,ed->re", out_grad, w_message, preferred_element_type=jnp.float32)
        / degree[:, None]
    ).astype(jnp.bfloat16)
    slot_grads = jnp.dot(edge_counts, dmessage, preferred_element_type=jnp.float32).astype(
        jnp.bfloat16
    )
    returned = lax.all_to_all(
        slot_grads.reshape(peer_count, slot_count, feat_width),
        "dom",
        split_axis=0,
        concat_axis=0,
        tiled=True,
    )
    returned = jnp.where(live_slots[:, :, None], returned.astype(jnp.float32), 0.0)
    halo_grad = jax.ops.segment_sum(
        returned.reshape(peer_count * slot_count, feat_width), send_rows.reshape(-1), row_count
    )
    dnormed = jnp.einsum("rd,ed->re", dquery, w_query, preferred_element_type=jnp.float32)
    dnormed = dnormed + jnp.einsum("rd,ed->re", dkey, w_key, preferred_element_type=jnp.float32)
    dnormed = dnormed + jnp.einsum("rd,ed->re", dvalue, w_value, preferred_element_type=jnp.float32)
    dnormed = dnormed + halo_grad
    dfeatures, gain_term = norm_pull(dnormed)
    feature_grad = (out_grad.astype(jnp.float32) + dfeatures).astype(jnp.bfloat16)
    weight_terms = jnp.stack(
        [
            jnp.einsum("rd,re->de", normed, dquery, preferred_element_type=jnp.float32),
            jnp.einsum("rd,re->de", normed, dkey, preferred_element_type=jnp.float32),
            jnp.einsum("rd,re->de", normed, dvalue, preferred_element_type=jnp.float32),
            jnp.einsum("rd,re->de", attn_rows, out_grad, preferred_element_type=jnp.float32),
            jnp.einsum("rd,re->de", mean_rows, out_grad, preferred_element_type=jnp.float32),
        ]
    )
    weight_sums, gain_sum = lax.psum((weight_terms, gain_term), ("dom", "blk"))
    return (layer_out, feature_grad, weight_sums, gain_sum)


def solution(mesh):
    placed = (
        P(("dom", "blk"), None),
        P(),
        P(),
        P(),
        P(),
        P(),
        P(),
        P(("dom", "blk")),
        P(("dom", "blk"), None),
        P(("dom", "blk"), None),
        P(("dom", "blk")),
        P(("dom", "blk")),
        P(("dom", "blk")),
        P(("dom", "blk"), None),
    )
    return jax.shard_map(
        local,
        mesh=mesh,
        in_specs=placed,
        out_specs=(P(("dom", "blk"), None), P(("dom", "blk"), None), P(), P()),
        check_vma=False,
    )
```

profile of v0, /device:TPU:1, one launch (start us, length us, event | category | flops | bytes accessed | tf_op | source)
XLA Modules:
  0.0 467.6 jit_solution(4525256311109926087)
XLA Ops:
  15.0 2.1 copy.152
  18.3 13.1 %all-gather = s32[8,1,256]{2,1,0:T(1,128)S(1)} all-gather(s32[1,1,256]{2,1,0:T(1,128)S(1)} %bitcast.258), channel_id=1, replica_groups=mesh['dom'=16,'blk'=8] {'blk'}, dimensions={0}, use_global_device_ids=true | all-gather | bytes 9216 | tf_op jit(solution)/shard_map/all_gather | solution.py:156
  33.6 7.9 %all-gather.6.cloned.1.call-done = bf16[2048,512]{1,0:T(8,128)(2,1)} async-done(((bf16[256,512]{1,0:T(8,128)(2,1)}), bf16[2048,512]{1,0:T(8,128)(2,1)}) %all-gather.6.cloned.1.call-update) | async-done | bytes 2097168 | tf_op jit(solution)/shard_map/all_gather | solution.py:154
  41.5 2.5 fusion.54
  43.9 1.8 copy.156
  45.7 23.3 %all-gather.4.cloned.1.call-done = bf16[2048,512]{1,0:T(8,128)(2,1)} async-done(((bf16[256,512]{1,0:T(8,128)(2,1)}), bf16[2048,512]{1,0:T(8,128)(2,1)}) %all-gather.4.cloned.1.call-update) | async-done | bytes 2097168 | tf_op jit(solution)/shard_map/all_gather | solution.py:155
  69.0 2.8 fusion.55
  71.9 1.8 copy.150
  83.3 1.8 copy.174
  101.9 6.1 %reshape.794 = bf16[8,256,8,64]{3,2,1,0:T(8,128)(2,1)} reshape(bf16[2048,512]{1,0:T(8,128)(2,1)} %all-gather.6.cloned.1.call-done) | data formatting | bytes 4194304 | tf_op jit(solution)/shard_map/reshape | solution.py:182
  108.0 5.1 %copy.182 = bf16[8,256,8,64]{1,3,2,0:T(8,128)(2,1)} copy(bf16[8,256,8,64]{3,2,1,0:T(8,128)(2,1)} %reshape.794) | data formatting | bytes 4194304
  113.1 6.1 %reshape.795 = bf16[8,256,8,64]{3,2,1,0:T(8,128)(2,1)} reshape(bf16[2048,512]{1,0:T(8,128)(2,1)} %all-gather.4.cloned.1.call-done) | data formatting | bytes 4194304 | tf_op jit(solution)/shard_map/reshape | solution.py:183
  119.3 5.1 %copy.183 = bf16[8,256,8,64]{1,3,2,0:T(8,128)(2,1)} copy(bf16[8,256,8,64]{3,2,1,0:T(8,128)(2,1)} %reshape.795) | data formatting | bytes 4194304
  124.4 67.0 %while.17 = (s32[]{:T(128)}, f32[256,8,64]{0,2,1:T(8,128)S(1)}, bf16[8,256,512]{1,2,0:T(8,128)(2,1)}, bf16[8,256,512]{2,1,0:T(8,128)(2,1)}, bf16[8,256,8,64]{1,3...) while((s32[]{:T(128)}, f32[256,8,64]{0,2,1:T(8,128)S(1)}, ...), condition=%wide.region_23.24_spmd.clone, body=%wide.region_22.23_spmd.clone.sunk | while | flops 340262912 | bytes 15088305 | solution.py:188
  191.4 4.0 copy.184
  196.1 7.5 %gather_fusion = bf16[2048,512]{1,0:T(8,128)(2,1)S(1)} fusion(bf16[256,512]{1,0:T(8,128)(2,1)S(1)} %fusion.38, s32[2048]{0:T(1024)S(1)} %fusion.48), kind=kCustom, calls=%fused_computation | custom fusion | bytes 4202496 | tf_op jit(solution)/shard_map/gather | solution.py:130
  205.2 6.6 %all-to-all-start = ((bf16[16,128,512]{2,1,0:T(8,128)(2,1)}), bf16[16,128,512]{2,1,0:T(8,128)(2,1)}, u32[]{:S(2)}, u32[]{:S(2)}) async-start(bf16[16,128,512]{2,1,0:T(8,128)(2,1)} %broadcast_select_fusion), calls=%async_computation | async-start | bytes 4194304 | tf_op jit(solution)/shard_map/all_to_all | solution.py:131
  212.6 22.4 %scatter_custom_fusion = s32[524288]{0:T(1024)S(1)} fusion(s32[4096]{0:T(1024)S(1)} %compare_select_fusion, s32[4096]{0:T(1024)S(1)} %broadcast.736, s32[]{:T(128)} %constant.148.clone.1), kind=kCustom, calls=%fused_computation.77 | custom fusion | flops 4096 | bytes 2097156 | tf_op jit(solution)/shard_map/scatter-add | solution.py:161
  237.6 28.8 %scatter_custom_fusion.1 = f32[256]{0:T(256)S(1)} fusion(s32[4096]{0:T(1024)S(1)} %copy-done.48, f32[4096]{0:T(1024)S(1)} %broadcast.737, f32[]{:T(128)} %constant.152.clone.1), kind=kCustom, calls=%fused_computation.188 | custom fusion | flops 4096 | bytes 1028 | tf_op jit(solution)/shard_map/scatter-add | solution.py:164
  266.4 2.4 convolution_convert_fusion
  268.8 6.6 %all-to-all-start.1 = ((bf16[16,128,512]{2,1,0:T(8,128)(2,1)}), bf16[16,128,512]{2,1,0:T(8,128)(2,1)S(1)}, u32[]{:S(2)}, u32[]{:S(2)}) async-start(bf16[16,128,512]{2,1,0:T(8,128)(2,1)} %bitcast.233), calls=%async_computation.3 | async-start | bytes 4194304 | tf_op jit(solution)/shard_map/all_to_all | solution.py:216
  275.4 3.4 fusion.21
  281.1 2.0 convert_multiply_fusion.4
  283.1 2.1 copy.186
  287.1 2.0 copy.187
  292.7 2.3 fusion.16
  299.7 2.5 all-to-all-done.1
  302.2 2.5 convert_select_fusion
  306.9 13.5 %scatter_fusion = f32[256,512]{1,0:T(8,128)S(1)} fusion(f32[256,512]{1,0:T(8,128)S(1)} %convolution_add_fusion.7, s32[2048]{0:T(1024)S(1)} %bitcast.259, f32[2048,512]{1,0:T(8,128)} %bitcast.218), kind=kCustom, calls=%fused_computation.3 | custom fusion | flops 1048576 | bytes 12591104 | tf_op jit(solution)/shard_map/scatter-add | solution.py:224
  320.6 65.8 %psum.15 = f32[512]{0:T(512)} all-reduce(f32[512]{0:T(512)S(1)} %get-tuple-element.245), channel_id=1, replica_groups=mesh['dom'=16,'blk'=8] {'dom','blk'}, use_global_device_ids=true, to_apply=%region_32.33 | all-reduce | flops 512 | bytes 4096 | tf_op jit(solution)/shard_map/psum | solution.py:242
  387.3 67.9 %all-reduce.2.cloned.1.call-done = f32[5,512,512]{2,1,0:T(8,128)} async-done(((f32[5,512,512]{2,1,0:T(8,128)}), f32[5,512,512]{2,1,0:T(8,128)}) %all-reduce.2.cloned.1.call-update) | async-done | bytes 5242896 | tf_op jit(solution)/shard_map/psum | solution.py:242
  455.3 5.8 %copy.248 = f32[5,512,512]{2,1,0:T(8,128)} copy(f32[5,512,512]{2,1,0:T(8,128)} %all-reduce.2.cloned.1.call-done) | data formatting | bytes 10485760
  (309 shorter events, 119.3 us)
Async XLA Ops:
  7.2 259.2 %copy-start = (bf16[512,512]{1,0:T(8,128)(2,1)S(1)}, bf16[512,512]{1,0:T(8,128)(2,1)}, u32[]{:S(2)}) copy-start(bf16[512,512]{1,0:T(8,128)(2,1)} %param.22) | copy-start | bytes 1572868
  7.2 34.3 %all-gather.6.cloned.1.call-start = ((), (), s32[]{:S(2)}) async-start(), calls=%async_computation.5 | async-start | bytes 2359296 | tf_op jit(solution)/shard_map/all_gather | solution.py:154
  11.1 2.3 copy-start.21
  11.4 2.1 copy-start.6
  12.3 56.8 %all-gather.4.cloned.1.call-start = ((), (), s32[]{:S(2)}) async-start(), calls=%async_computation.4 | async-start | bytes 2359296 | tf_op jit(solution)/shard_map/all_gather | solution.py:155
  13.4 267.7 %reduce-scatter.3.cloned.1.call-start = ((), (), s32[]{:S(2)}) async-start(), calls=%async_computation.6 | async-start | bytes 2359296 | tf_op jit(solution)/shard_map/reduce_scatter | solution.py:192
  14.0 3.1 copy-start.3
  14.0 4.3 copy-start.44
  14.0 17.5 %copy-start.49 = (s32[1,8]{1,0:T(1,128)S(1)}, s32[1,8]{1,0:T(1,128)}, u32[]{:S(2)}) copy-start(s32[1,8]{1,0:T(1,128)} %param.24) | copy-start | bytes 100
  14.1 19.2 %copy-start.7 = (bf16[256,512]{1,0:T(8,128)(2,1)S(1)}, bf16[256,512]{1,0:T(8,128)(2,1)}, u32[]{:S(2)}) copy-start(bf16[256,512]{1,0:T(8,128)(2,1)} %param.29) | copy-start | bytes 786436
  14.1 19.2 %copy-start.17 = (bf16[512,512]{1,0:T(8,128)(2,1)S(1)}, bf16[512,512]{1,0:T(8,128)(2,1)}, u32[]{:S(2)}) copy-start(bf16[512,512]{1,0:T(8,128)(2,1)} %param.21) | copy-start | bytes 1572868
  90.5 1.8 copy-start.24
  90.5 2.1 copy-start.37
  90.5 2.1 copy-start.43
  196.1 7.5 %copy-start.50 = (s32[16]{0:T(128)S(1)}, s32[16]{0:T(128)}, u32[]{:S(2)}) copy-start(s32[16]{0:T(128)} %param.26) | copy-start | bytes 196
  205.2 63.5 %all-to-all-start = ((bf16[16,128,512]{2,1,0:T(8,128)(2,1)}), bf16[16,128,512]{2,1,0:T(8,128)(2,1)}, u32[]{:S(2)}, u32[]{:S(2)}) async-start(bf16[16,128,512]{2,1,0:T(8,128)(2,1)} %broadcast_select_fusion), calls=%async_computation | async-start | bytes 4194304 | tf_op jit(solution)/shard_map/all_to_all | solution.py:131
  211.8 80.8 %reduce-scatter.5.cloned.1.call-start = ((), (), s32[]{:S(2)}) async-start(), calls=%async_computation.7 | async-start | bytes 2359296 | tf_op jit(solution)/shard_map/reduce_scatter | solution.py:198
  236.1 30.3 %copy-start.8 = (bf16[256,512]{1,0:T(8,128)(2,1)S(1)}, bf16[256,512]{1,0:T(8,128)(2,1)}, u32[]{:S(2)}) copy-start(bf16[256,512]{1,0:T(8,128)(2,1)} %param.29) | copy-start | bytes 786436
  237.5 31.2 %copy-start.25 = (bf16[2048,256]{1,0:T(8,128)(2,1)}, bf16[2048,256]{1,0:T(8,128)(2,1)S(1)}, u32[]{:S(2)}) copy-start(bf16[2048,256]{1,0:T(8,128)(2,1)S(1)} %convert_element_type.131) | copy-start | bytes 3145732
  268.8 33.4 %all-to-all-start.1 = ((bf16[16,128,512]{2,1,0:T(8,128)(2,1)}), bf16[16,128,512]{2,1,0:T(8,128)(2,1)S(1)}, u32[]{:S(2)}, u32[]{:S(2)}) async-start(bf16[16,128,512]{2,1,0:T(8,128)(2,1)} %bitcast.233), calls=%async_computation.3 | async-start | bytes 4194304 | tf_op jit(solution)/shard_map/all_to_all | solution.py:216
  275.4 179.9 %all-reduce.2.cloned.1.call-start = ((), (), s32[]{:S(2)}) async-start(), calls=%async_computation.8 | async-start | bytes 10485760 | tf_op jit(solution)/shard_map/psum | solution.py:242
  275.4 3.4 copy-start.4
  281.1 8.1 %copy-start.2 = (f32[256,512]{1,0:T(8,128)S(1)}, f32[256,512]{1,0:T(8,128)}, u32[]{:S(2)}) copy-start(f32[256,512]{1,0:T(8,128)} %copy-done.1) | copy-start | bytes 1572868
  291.4 3.6 copy-start.9
  291.4 3.6 copy-start.27
  292.7 3.6 copy-start.28
  299.7 5.1 %copy-start.12 = (bf16[256,8,64]{0,2,1:T(8,128)(2,1)S(1)}, bf16[256,8,64]{0,2,1:T(8,128)(2,1)}, u32[]{:S(2)}) copy-start(bf16[256,8,64]{0,2,1:T(8,128)(2,1)} %copy-done.11) | copy-start | bytes 786436
  302.2 2.5 copy-start.22
  302.2 2.9 copy-start.16
  302.2 2.9 copy-start.18
  306.9 13.6 %copy-start.46 = (f32[512]{0:T(512)S(1)}, f32[512]{0:T(512)}, u32[]{:S(2)}) copy-start(f32[512]{0:T(512)} %param.17) | copy-start | bytes 6148
  306.9 79.6 %copy-start.10 = (bf16[256,512]{1,0:T(8,128)(2,1)S(1)}, bf16[256,512]{1,0:T(8,128)(2,1)}, u32[]{:S(2)}) copy-start(bf16[256,512]{1,0:T(8,128)(2,1)} %param.29) | copy-start | bytes 786436
  (26 other events, 27.3 us)
Sparse Core Ops, SparseCore 0:
  12.4 29.0 all-gather.5
  43.2 25.8 all-gather.3
  195.5 30.9 reduce-scatter.2
  228.8 32.8 reduce-scatter.4
  297.7 157.5 all-reduce.1
where the time goes:
time: 470 us; the launch traced here: 468 us
  waiting for transfers between devices  102 us (22%)
  local copies, waits for them, and re-layouts  97.6 us (21%)
  other arithmetic  84.2 us (18%)
  blocking collectives  78.9 us (17%)
  matrix products  70.8 us (15%)
  between operations  14.7 us (3%)
  starting transfers between devices  13.4 us (3%)
  loops' own time  5.81 us (1%)
    psum x1, waiting for transfers between devices, local(): weight_sums, gain_sum = lax.psum((weight_terms, gain_term), ('dom', 'blk'))  67.9 us
    psum x1, blocking collectives, local(): weight_sums, gain_sum = lax.psum((weight_terms, gain_term), ('dom', 'blk'))  65.8 us
    scatter-add x1, other arithmetic, local(): jax.ops.segment_sum(jnp.ones(edge_dst.shape, jnp.float32), edge_dst, row_...  28.8 us
    all_gather x1, waiting for transfers between devices, local(): lax.all_gather(value_flat, 'blk', axis=0, tiled=True)  23.3 us
    scatter-add x1, other arithmetic, local(): jnp.zeros((peer_count * slot_count * row_count,), jnp.int32).at[pair_index]  22.4 us
    unnamed x106, local copies, waits for them, and re-layouts  20.3 us
    dot_general x16, matrix products, block_weights(): jnp.einsum('rhe,khe->hrk', query_heads, key_heads, preferred_element_type...  19.7 us
    slice x9, local copies, waits for them, and re-layouts, attend_piece(): value_rows[first_row:last_row].reshape(part_rows, HEADS, HEAD_DIM)  13.6 us
  transfers between devices with their start and end apart: 7, of which 4 were waited for; matrix products, arithmetic and copies ran while one was open for 25% of the time, Pallas kernels for 0%

commit v1 on v0

--- a/solution.py
+++ b/solution.py
@@ -150,9 +150,29 @@
         skip_empty=False,
     )
     key_set = None
+
+    def leaves_return_all(a0, dim_k):
+        chips = jax.lax.axis_size("blk")
+        current_block = range(chips)
+        far_arr = map(lambda num: (num, (num + 1) % chips), current_block)
+        table = list(far_arr)
+        ready = range(chips)
+        before = map(lambda num: (num, (num - 1) % chips), ready)
+        found = list(before)
+        tall, o_now = ([a0], [a0])
+        for _ in range(chips // 2):
+            k_now = jax.lax.ppermute(tall[-1], "blk", table)
+            tall.append(k_now)
+        for _ in [*range((chips - 1) // 2)]:
+            b_now = jax.lax.ppermute(o_now[-1], "blk", found)
+            o_now.append(b_now)
+        carry_out = jnp.concatenate([*tall[::-1], *o_now[1:]], dim_k)
+        main = jax.lax.axis_index("blk")
+        return jnp.roll(carry_out, (main - chips // 2) * a0.shape[dim_k], dim_k)
+
     key_set = (
         lax.all_gather(key_flat, "blk", axis=0, tiled=True),
-        lax.all_gather(value_flat, "blk", axis=0, tiled=True),
+        leaves_return_all(value_flat, 0),
         lax.all_gather(node_cluster, "blk", axis=0, tiled=True),
     )
     numer, denom = fold_step(start_state, key_set, 0)

time: 470 us -> 476 us (1.013)
  waiting for transfers between devices: 102 us -> 76.8 us
  local copies, waits for them, and re-layouts: 97.6 us -> 111 us
  starting transfers between devices: 13.4 us -> 23.8 us
    all_gather x1 -> x0, waiting for transfers between devices: 23.3 us -> none  [local(): lax.all_gather(value_flat, 'blk', axis=0, tiled=True)]
    unnamed x106 -> x129, local copies, waits for them, and re-layouts: 20.3 us -> 32 us
    ppermute x0 -> x7, starting transfers between devices: none -> 10.5 us  [the longest x4 7.28 us: leaves_return_all(): k_now = jax.lax.ppermute(tall[-1], 'blk', table)]
    all_gather x1, waiting for transfers between devices: 7.86 us -> 0.01 us  [local(): lax.all_gather(key_flat, 'blk', axis=0, tiled=True)]
    ppermute x0 -> x7, waiting for transfers between devices: none -> 7.73 us  [the longest x4 7.73 us: leaves_return_all(): k_now = jax.lax.ppermute(tall[-1], 'blk', table)]
  transfers between devices with their start and end apart: 7 -> 13, of which waited for: 4 -> 2; matrix products, arithmetic and copies ran while one was open for 25% -> 33% of each run, Pallas kernels for 0% -> 0%
where the time goes in v1:
time: 476 us; the launch traced here: 473 us
  local copies, waits for them, and re-layouts  111 us (23%)
  other arithmetic  88.7 us (19%)
  blocking collectives  81.7 us (17%)
  waiting for transfers between devices  76.8 us (16%)
  matrix products  70 us (15%)
  starting transfers between devices  23.8 us (5%)
  between operations  14.9 us (3%)
  loops' own time  5.81 us (1%)
    psum x1, blocking collectives, local(): weight_sums, gain_sum = lax.psum((weight_terms, gain_term), ('dom', 'blk'))  69.8 us
    psum x1, waiting for transfers between devices, local(): weight_sums, gain_sum = lax.psum((weight_terms, gain_term), ('dom', 'blk'))  68.3 us
    unnamed x129, local copies, waits for them, and re-layouts  32 us
    scatter-add x1, other arithmetic, local(): jax.ops.segment_sum(jnp.ones(edge_dst.shape, jnp.float32), edge_dst, row_...  28.8 us
    scatter-add x1, other arithmetic, local(): jnp.zeros((peer_count * slot_count * row_count,), jnp.int32).at[pair_index]  22.4 us
    dot_general x16, matrix products, block_weights(): jnp.einsum('rhe,khe->hrk', query_heads, key_heads, preferred_element_type...  19.7 us
    slice x9, local copies, waits for them, and re-layouts, attend_piece(): key_part = key_rows[first_row:last_row].reshape(part_rows, HEADS, HEAD_DIM)  14.1 us
    scatter-add x1, other arithmetic, local(): jax.ops.segment_sum(returned.reshape(peer_count * slot_count, feat_width)...  13.4 us
  transfers between devices with their start and end apart: 13, of which 2 were waited for; matrix products, arithmetic and copies ran while one was open for 33% of the time, Pallas kernels for 0%

profile of v1, /device:TPU:1, one launch (start us, length us, event | category | flops | bytes accessed | tf_op | source)
XLA Modules:
  0.0 473.2 jit_solution(1638827338240900291)
XLA Ops:
  10.9 3.0 collective-permute-start
  20.3 11.9 %all-gather = s32[8,1,256]{2,1,0:T(1,128)S(1)} all-gather(s32[1,1,256]{2,1,0:T(1,128)S(1)} %bitcast.258), channel_id=1, replica_groups=mesh['dom'=16,'blk'=8] {'blk'}, dimensions={0}, use_global_device_ids=true | all-gather | bytes 9216 | tf_op jit(solution)/shard_map/all_gather | solution.py:176
  32.3 7.7 %collective-permute-done.1 = bf16[256,512]{1,0:T(8,128)(2,1)} collective-permute-done((bf16[256,512]{1,0:T(8,128)(2,1)}, bf16[256,512]{1,0:T(8,128)(2,1)}, u32[]{:S(2)}, u32[]{:S(2)}) %collective-permute-start.1) | collective-permute-done | bytes 262176 | tf_op jit(solution)/shard_map/ppermute | solution.py:164
  40.1 2.5 collective-permute-start.2
  48.6 2.2 compare_and_fusion.1
  52.4 2.2 collective-permute-start.6
  67.9 1.8 copy.149
  71.5 1.8 copy.163
  76.1 3.1 constant_dynamic-slice_fusion.9
  79.1 6.1 %reshape.795 = bf16[8,256,8,64]{3,2,1,0:T(8,128)(2,1)} reshape(bf16[2048,512]{1,0:T(8,128)(2,1)} %constant_dynamic-slice_fusion.9) | data formatting | bytes 4194304 | tf_op jit(solution)/shard_map/reshape | solution.py:203
  85.3 5.2 %copy.182 = bf16[8,256,8,64]{1,3,2,0:T(8,128)(2,1)} copy(bf16[8,256,8,64]{3,2,1,0:T(8,128)(2,1)} %reshape.795) | data formatting | bytes 4194304
  90.4 2.6 fusion.54
  116.8 6.1 %reshape.794 = bf16[8,256,8,64]{3,2,1,0:T(8,128)(2,1)} reshape(bf16[2048,512]{1,0:T(8,128)(2,1)} %all-gather.3.cloned.1.call-done) | data formatting | bytes 4194304 | tf_op jit(solution)/shard_map/reshape | solution.py:202
  123.0 5.1 %copy.181 = bf16[8,256,8,64]{1,3,2,0:T(8,128)(2,1)} copy(bf16[8,256,8,64]{3,2,1,0:T(8,128)(2,1)} %reshape.794) | data formatting | bytes 4194304
  128.1 67.0 %while.17 = (s32[]{:T(128)}, f32[256,8,64]{0,2,1:T(8,128)S(1)}, bf16[8,256,512]{1,2,0:T(8,128)(2,1)}, bf16[8,256,512]{2,1,0:T(8,128)(2,1)}, bf16[8,256,8,64]{1,3...) while((s32[]{:T(128)}, f32[256,8,64]{0,2,1:T(8,128)S(1)}, ...), condition=%wide.region_23.24_spmd.clone, body=%wide.region_22.23_spmd.clone.sunk | while | flops 340262912 | bytes 15088305 | solution.py:208
  195.0 4.2 copy.183
  199.9 7.5 %gather_fusion = bf16[2048,512]{1,0:T(8,128)(2,1)S(1)} fusion(bf16[256,512]{1,0:T(8,128)(2,1)S(1)} %fusion.38, s32[2048]{0:T(1024)S(1)} %fusion.48), kind=kCustom, calls=%fused_computation | custom fusion | bytes 4202496 | tf_op jit(solution)/shard_map/gather | solution.py:130
  209.0 6.6 %all-to-all-start = ((bf16[16,128,512]{2,1,0:T(8,128)(2,1)}), bf16[16,128,512]{2,1,0:T(8,128)(2,1)}, u32[]{:S(2)}, u32[]{:S(2)}) async-start(bf16[16,128,512]{2,1,0:T(8,128)(2,1)} %broadcast_select_fusion), calls=%async_computation | async-start | bytes 4194304 | tf_op jit(solution)/shard_map/all_to_all | solution.py:131
  216.4 22.4 %scatter_custom_fusion = s32[524288]{0:T(1024)S(1)} fusion(s32[4096]{0:T(1024)S(1)} %compare_select_fusion, s32[4096]{0:T(1024)S(1)} %broadcast.737, s32[]{:T(128)} %constant.171.clone.1), kind=kCustom, calls=%fused_computation.77 | custom fusion | flops 4096 | bytes 2097156 | tf_op jit(solution)/shard_map/scatter-add | solution.py:181
  241.5 28.8 %scatter_custom_fusion.1 = f32[256]{0:T(256)S(1)} fusion(s32[4096]{0:T(1024)S(1)} %copy-done.52, f32[4096]{0:T(1024)S(1)} %broadcast.738, f32[]{:T(128)} %constant.175.clone.1), kind=kCustom, calls=%fused_computation.213 | custom fusion | flops 4096 | bytes 1028 | tf_op jit(solution)/shard_map/scatter-add | solution.py:184
  270.3 2.4 convolution_convert_fusion
  272.6 6.6 %all-to-all-start.1 = ((bf16[16,128,512]{2,1,0:T(8,128)(2,1)}), bf16[16,128,512]{2,1,0:T(8,128)(2,1)S(1)}, u32[]{:S(2)}, u32[]{:S(2)}) async-start(bf16[16,128,512]{2,1,0:T(8,128)(2,1)} %bitcast.233), calls=%async_computation.3 | async-start | bytes 4194304 | tf_op jit(solution)/shard_map/all_to_all | solution.py:236
  279.3 3.4 fusion.21
  284.9 2.1 convert_multiply_fusion.4
  287.0 2.1 copy.185
  291.1 2.1 copy.186
  296.6 2.3 fusion.16
  303.7 2.3 convert_select_fusion
  308.2 13.4 %scatter_fusion = f32[256,512]{1,0:T(8,128)S(1)} fusion(f32[256,512]{1,0:T(8,128)S(1)} %convolution_add_fusion.7, s32[2048]{0:T(1024)S(1)} %bitcast.259, f32[2048,512]{1,0:T(8,128)} %bitcast.218), kind=kCustom, calls=%fused_computation.3 | custom fusion | flops 1048576 | bytes 12591104 | tf_op jit(solution)/shard_map/scatter-add | solution.py:244
  321.8 69.8 %psum.15 = f32[512]{0:T(512)} all-reduce(f32[512]{0:T(512)S(1)} %get-tuple-element.245), channel_id=1, replica_groups=mesh['dom'=16,'blk'=8] {'dom','blk'}, use_global_device_ids=true, to_apply=%region_32.33 | all-reduce | flops 512 | bytes 4096 | tf_op jit(solution)/shard_map/psum | solution.py:262
  392.6 68.3 %all-reduce.2.cloned.1.call-done = f32[5,512,512]{2,1,0:T(8,128)} async-done(((f32[5,512,512]{2,1,0:T(8,128)}), f32[5,512,512]{2,1,0:T(8,128)}) %all-reduce.2.cloned.1.call-update) | async-done | bytes 5242896 | tf_op jit(solution)/shard_map/psum | solution.py:262
  460.8 5.8 %copy.262 = f32[5,512,512]{2,1,0:T(8,128)} copy(f32[5,512,512]{2,1,0:T(8,128)} %all-reduce.2.cloned.1.call-done) | data formatting | bytes 10485760
  (345 shorter events, 141.2 us)
Async XLA Ops:
  7.2 263.1 %copy-start = (bf16[512,512]{1,0:T(8,128)(2,1)S(1)}, bf16[512,512]{1,0:T(8,128)(2,1)}, u32[]{:S(2)}) copy-start(bf16[512,512]{1,0:T(8,128)(2,1)} %param.22) | copy-start | bytes 1572868
  7.2 6.7 %copy-start.16 = (bf16[512,512]{1,0:T(8,128)(2,1)S(1)}, bf16[512,512]{1,0:T(8,128)(2,1)}, u32[]{:S(2)}) copy-start(bf16[512,512]{1,0:T(8,128)(2,1)} %param.19) | copy-start | bytes 1572868
  7.2 83.2 %all-gather.3.cloned.1.call-start = ((), (), s32[]{:S(2)}) async-start(), calls=%async_computation.4 | async-start | bytes 2359296 | tf_op jit(solution)/shard_map/all_gather | solution.py:174
  10.9 21.4 %collective-permute-start = (bf16[256,512]{1,0:T(8,128)(2,1)S(1)}, bf16[256,512]{1,0:T(8,128)(2,1)}, u32[]{:S(2)}, u32[]{:S(2)}) collective-permute-start(bf16[256,512]{1,0:T(8,128)(2,1)S(1)} %convolution_convert_fusion.1), channel_id=1, source_target_pairs={{0,1},{1,2},{2,3},{3,4},{4,5},{5,6},{6,7},{7,0},{8,9},{9,10},{10,1... | collective-permute-start | bytes 786440 | tf_op jit(solution)/shard_map/ppermute | solution.py:164
  13.9 32.0 %collective-permute-start.4 = (bf16[256,512]{1,0:T(8,128)(2,1)S(1)}, bf16[256,512]{1,0:T(8,128)(2,1)}, u32[]{:S(2)}, u32[]{:S(2)}) collective-permute-start(bf16[256,512]{1,0:T(8,128)(2,1)S(1)} %convolution_convert_fusion.1), channel_id=1, source_target_pairs={{0,7},{1,0},{2,1},{3,2},{4,3},{5,4},{6,5},{7,6},{8,15},{9,8},{10,9... | collective-permute-start | bytes 786440 | tf_op jit(solution)/shard_map/ppermute | solution.py:167
  14.4 4.8 %copy-start.22 = (bf16[512,512]{1,0:T(8,128)(2,1)S(1)}, bf16[512,512]{1,0:T(8,128)(2,1)}, u32[]{:S(2)}) copy-start(bf16[512,512]{1,0:T(8,128)(2,1)} %param.18) | copy-start | bytes 1572868
  14.8 3.9 copy-start.7
  14.8 5.6 %copy-start.48 = (s32[256]{0:T(256)S(1)}, s32[256]{0:T(256)}, u32[]{:S(2)}) copy-start(s32[256]{0:T(256)} %param.23) | copy-start | bytes 3076
  15.7 269.3 %reduce-scatter.3.cloned.1.call-start = ((), (), s32[]{:S(2)}) async-start(), calls=%async_computation.5 | async-start | bytes 2359296 | tf_op jit(solution)/shard_map/reduce_scatter | solution.py:212
  20.3 30.6 %copy-start.3 = (f32[256,512]{0,1:T(8,128)}, f32[256,512]{0,1:T(8,128)S(1)}, u32[]{:S(2)}) copy-start(f32[256,512]{0,1:T(8,128)S(1)} %copy.150) | copy-start | bytes 1572868
  32.2 7.8 %collective-permute-start.1 = (bf16[256,512]{1,0:T(8,128)(2,1)}, bf16[256,512]{1,0:T(8,128)(2,1)}, u32[]{:S(2)}, u32[]{:S(2)}) collective-permute-start(bf16[256,512]{1,0:T(8,128)(2,1)} %collective-permute-done), channel_id=1, source_target_pairs={{0,1},{1,2},{2,3},{3,4},{4,5},{5,6},{6,7},{7,0},{8,9},{9,10},{10,1... | collective-permute-start | bytes 786440 | tf_op jit(solution)/shard_map/ppermute | solution.py:164
  32.3 19.7 %copy-start.8 = (bf16[256,512]{1,0:T(8,128)(2,1)S(1)}, bf16[256,512]{1,0:T(8,128)(2,1)}, u32[]{:S(2)}) copy-start(bf16[256,512]{1,0:T(8,128)(2,1)} %param.29) | copy-start | bytes 786436
  32.3 19.7 %copy-start.19 = (bf16[512,512]{1,0:T(8,128)(2,1)S(1)}, bf16[512,512]{1,0:T(8,128)(2,1)}, u32[]{:S(2)}) copy-start(bf16[512,512]{1,0:T(8,128)(2,1)} %param.21) | copy-start | bytes 1572868
  40.1 6.8 %collective-permute-start.2 = (bf16[256,512]{1,0:T(8,128)(2,1)}, bf16[256,512]{1,0:T(8,128)(2,1)}, u32[]{:S(2)}, u32[]{:S(2)}) collective-permute-start(bf16[256,512]{1,0:T(8,128)(2,1)} %collective-permute-done.1), channel_id=1, source_target_pairs={{0,1},{1,2},{2,3},{3,4},{4,5},{5,6},{6,7},{7,0},{8,9},{9,10},{10,1... | collective-permute-start | bytes 786440 | tf_op jit(solution)/shard_map/ppermute | solution.py:164
  45.9 6.5 %collective-permute-start.5 = (bf16[256,512]{1,0:T(8,128)(2,1)}, bf16[256,512]{1,0:T(8,128)(2,1)S(1)}, u32[]{:S(2)}, u32[]{:S(2)}) collective-permute-start(bf16[256,512]{1,0:T(8,128)(2,1)} %collective-permute-done.4), channel_id=1, source_target_pairs={{0,7},{1,0},{2,1},{3,2},{4,3},{5,4},{6,5},{7,6},{8,15},{9,8},{10,9... | collective-permute-start | bytes 786440 | tf_op jit(solution)/shard_map/ppermute | solution.py:167
  46.9 7.7 %collective-permute-start.3 = (bf16[256,512]{1,0:T(8,128)(2,1)}, bf16[256,512]{1,0:T(8,128)(2,1)}, u32[]{:S(2)}, u32[]{:S(2)}) collective-permute-start(bf16[256,512]{1,0:T(8,128)(2,1)} %collective-permute-done.2), channel_id=1, source_target_pairs={{0,1},{1,2},{2,3},{3,4},{4,5},{5,6},{6,7},{7,0},{8,9},{9,10},{10,1... | collective-permute-start | bytes 786440 | tf_op jit(solution)/shard_map/ppermute | solution.py:164
  52.4 7.1 %collective-permute-start.6 = (bf16[256,512]{1,0:T(8,128)(2,1)S(1)}, bf16[256,512]{1,0:T(8,128)(2,1)S(1)}, u32[]{:S(2)}, u32[]{:S(2)}) collective-permute-start(bf16[256,512]{1,0:T(8,128)(2,1)S(1)} %collective-permute-done.5), channel_id=1, source_target_pairs={{0,7},{1,0},{2,1},{3,2},{4,3},{5,4},{6,5},{7,6},{8,15},{9,8},{10,9... | collective-permute-start | bytes 786440 | tf_op jit(solution)/shard_map/ppermute | solution.py:167
  199.9 7.5 %copy-start.54 = (s32[16]{0:T(128)S(1)}, s32[16]{0:T(128)}, u32[]{:S(2)}) copy-start(s32[16]{0:T(128)} %param.26) | copy-start | bytes 196
  209.0 63.6 %all-to-all-start = ((bf16[16,128,512]{2,1,0:T(8,128)(2,1)}), bf16[16,128,512]{2,1,0:T(8,128)(2,1)}, u32[]{:S(2)}, u32[]{:S(2)}) async-start(bf16[16,128,512]{2,1,0:T(8,128)(2,1)} %broadcast_select_fusion), calls=%async_computation | async-start | bytes 4194304 | tf_op jit(solution)/shard_map/all_to_all | solution.py:131
  215.7 81.0 %reduce-scatter.5.cloned.1.call-start = ((), (), s32[]{:S(2)}) async-start(), calls=%async_computation.6 | async-start | bytes 2359296 | tf_op jit(solution)/shard_map/reduce_scatter | solution.py:218
  240.0 30.3 %copy-start.9 = (bf16[256,512]{1,0:T(8,128)(2,1)S(1)}, bf16[256,512]{1,0:T(8,128)(2,1)}, u32[]{:S(2)}) copy-start(bf16[256,512]{1,0:T(8,128)(2,1)} %param.29) | copy-start | bytes 786436
  241.4 31.2 %copy-start.29 = (bf16[2048,256]{1,0:T(8,128)(2,1)}, bf16[2048,256]{1,0:T(8,128)(2,1)S(1)}, u32[]{:S(2)}) copy-start(bf16[2048,256]{1,0:T(8,128)(2,1)S(1)} %convert_element_type.131) | copy-start | bytes 3145732
  272.6 31.1 %all-to-all-start.1 = ((bf16[16,128,512]{2,1,0:T(8,128)(2,1)}), bf16[16,128,512]{2,1,0:T(8,128)(2,1)S(1)}, u32[]{:S(2)}, u32[]{:S(2)}) async-start(bf16[16,128,512]{2,1,0:T(8,128)(2,1)} %bitcast.233), calls=%async_computation.3 | async-start | bytes 4194304 | tf_op jit(solution)/shard_map/all_to_all | solution.py:236
  279.2 181.6 %all-reduce.2.cloned.1.call-start = ((), (), s32[]{:S(2)}) async-start(), calls=%async_computation.7 | async-start | bytes 10485760 | tf_op jit(solution)/shard_map/psum | solution.py:262
  279.3 3.4 copy-start.4
  284.9 8.2 %copy-start.2 = (f32[256,512]{1,0:T(8,128)S(1)}, f32[256,512]{1,0:T(8,128)}, u32[]{:S(2)}) copy-start(f32[256,512]{1,0:T(8,128)} %copy-done.1) | copy-start | bytes 1572868
  295.3 3.6 copy-start.10
  295.3 3.6 copy-start.31
  296.6 3.6 copy-start.32
  303.7 2.7 copy-start.20
  308.1 13.5 %copy-start.50 = (f32[512]{0:T(512)S(1)}, f32[512]{0:T(512)}, u32[]{:S(2)}) copy-start(f32[512]{0:T(512)} %param.17) | copy-start | bytes 6148
  308.2 83.5 %copy-start.11 = (bf16[256,512]{1,0:T(8,128)(2,1)S(1)}, bf16[256,512]{1,0:T(8,128)(2,1)}, u32[]{:S(2)}) copy-start(bf16[256,512]{1,0:T(8,128)(2,1)} %param.29) | copy-start | bytes 786436
  (36 other events, 45.3 us)
Sparse Core Ops, SparseCore 0:
  15.8 28.4 all-gather.2
  199.3 33.8 reduce-scatter.2
  235.6 32.5 reduce-scatter.4
  301.7 159.1 all-reduce.1
